TPU v7x, 256 devices: a whole 4x4x8 slice. The times are simulated.
256 devices in a mesh: dist: 16 (over z_lo, y), rows: 16 (over z_hi, x, core).
Axes of the slice: x: 4, y: 4, z: 8 (z_hi: 2, z_lo: 4; z = z_hi * 4 + z_lo), core: 2. Of those that a mesh axis runs over, the one named last changes fastest.
Arguments:
- wave: float32 [16, 2, 2048, 2048], P('dist', None, 'rows'), may hold values from -6 to 6
- object_slice: float32 [2, 2048, 2048], P(None, 'rows', 'dist'), may hold values from 0 to 1.5
- fresnel: float32 [16], P('dist'), may hold values from 256 to 1024
Outputs:
- detected: float32 [16, 2, 2048, 2048], P('dist', None, 'rows')
All inputs are finite; a program needn't handle non-finite values.
Results may differ from a plain program's by a relative error of at most 0.00035.
Values sent between devices are 32-bit elements; how exact they have to be, the bound alone decides.
A program may use at most 64 MiB of HBM per device.

v0:
```python
import math
import jax
import jax.numpy as jnp
from jax import lax
from jax.sharding import PartitionSpec as P

highest = lax.Precision.HIGHEST


def swapped(shard, axis, apart):
    return lax.ppermute(shard, axis, [(i, i ^ 1 << apart) for i in range(lax.axis_size(axis))])


def angle_table(period, direction, row_count, col_count):
    row_grid = lax.broadcasted_iota(jnp.int32, (row_count, col_count), 0)
    col_grid = lax.broadcasted_iota(jnp.int32, (row_count, col_count), 1)
    phase_angle = (
        direction * 2.0 * math.pi / period * (row_grid * col_grid % period).astype(jnp.float32)
    )
    return (jnp.cos(phase_angle), jnp.sin(phase_angle))


def complex_mix(form, real_part, imag_part, table_re, table_im):
    out_re = jnp.einsum(form, real_part, table_re, precision=highest) - jnp.einsum(
        form, imag_part, table_im, precision=highest
    )
    out_im = jnp.einsum(form, real_part, table_im, precision=highest) + jnp.einsum(
        form, imag_part, table_re, precision=highest
    )
    return (out_re, out_im)


def split_length(length):
    levels = length.bit_length() - 1
    outer_len = 1 << (levels + 1) // 2
    return (outer_len, length // outer_len)


def transform_last(real_part, imag_part, direction):
    length = real_part.shape[-1]
    outer_len, inner_len = split_length(length)
    leading = real_part.shape[:-1]
    real_part = real_part.reshape(leading + (outer_len, inner_len))
    imag_part = imag_part.reshape(leading + (outer_len, inner_len))
    first_re, first_im = angle_table(outer_len, direction, outer_len, outer_len)
    real_part, imag_part = complex_mix("...ab,ae->...eb", real_part, imag_part, first_re, first_im)
    twiddle_re, twiddle_im = angle_table(length, direction, outer_len, inner_len)
    real_part, imag_part = (
        real_part * twiddle_re - imag_part * twiddle_im,
        real_part * twiddle_im + imag_part * twiddle_re,
    )
    last_re, last_im = angle_table(inner_len, direction, inner_len, inner_len)
    real_part, imag_part = complex_mix("...eb,bd->...de", real_part, imag_part, last_re, last_im)
    return (real_part.reshape(leading + (length,)), imag_part.reshape(leading + (length,)))


def signed_frequency(index_line, length):
    return (
        jnp.where(index_line < length // 2, index_line, index_line - length).astype(jnp.float32)
        / length
    )


def apply_kernel(real_part, imag_part, fresnel, row_index, col_index, length):
    row_freq = signed_frequency(row_index, length)
    col_freq = signed_frequency(col_index, length)
    freq_sum = row_freq[:, None] ** 2 + col_freq[None, :] ** 2
    phase_angle = (-math.pi * fresnel)[:, None, None] * freq_sum[None]
    kernel_re = jnp.cos(phase_angle)
    kernel_im = jnp.sin(phase_angle)
    return (
        real_part * kernel_re - imag_part * kernel_im,
        real_part * kernel_im + imag_part * kernel_re,
    )


def body(wave, object_slice, fresnel):
    row_count = wave.shape[2]
    length = wave.shape[3]
    group_size = lax.axis_size("rows")
    position = lax.axis_index("rows")
    slice_piece = lax.all_gather(object_slice, "dist", axis=2, tiled=True)
    amplitude = jnp.exp(-slice_piece[1])
    trans_re = amplitude * jnp.cos(slice_piece[0])
    trans_im = amplitude * jnp.sin(slice_piece[0])
    wave_re = wave[:, 0]
    wave_im = wave[:, 1]
    exited = jnp.stack(
        (wave_re * trans_re - wave_im * trans_im, wave_re * trans_im + wave_im * trans_re), axis=1
    )
    real_part, imag_part = transform_last(exited[:, 0], exited[:, 1], -1.0)
    rounds = group_size.bit_length() - 1
    for level in reversed(range(rounds)):
        stride = 1 << level
        partner = swapped(jnp.stack((real_part, imag_part), axis=1), "rows", level)
        upper_flag = (position // stride % 2).astype(jnp.float32)
        within = (position % stride).astype(jnp.float32)
        phase_angle = -2.0 * math.pi / (2 * stride) * within
        factor_re = 1.0 - upper_flag + upper_flag * jnp.cos(phase_angle)
        factor_im = upper_flag * jnp.sin(phase_angle)
        own_sign = 1.0 - 2.0 * upper_flag
        summed_re = partner[:, 0] + own_sign * real_part
        summed_im = partner[:, 1] + own_sign * imag_part
        real_part = summed_re * factor_re - summed_im * factor_im
        imag_part = summed_re * factor_im + summed_im * factor_re
    bit_reverse = jnp.zeros((), jnp.int32)
    for level in range(rounds):
        bit_reverse = bit_reverse + position // (1 << level) % 2 * (1 << rounds - 1 - level)
    local_rows = lax.iota(jnp.int32, row_count)
    shift_angle = -2.0 * math.pi / length * (local_rows * bit_reverse % length).astype(jnp.float32)
    shift_re = jnp.cos(shift_angle)[:, None]
    shift_im = jnp.sin(shift_angle)[:, None]
    real_part, imag_part = (
        real_part * shift_re - imag_part * shift_im,
        real_part * shift_im + imag_part * shift_re,
    )
    local_re, local_im = angle_table(row_count, -1.0, row_count, row_count)
    real_part, imag_part = complex_mix("...lc,lm->...mc", real_part, imag_part, local_re, local_im)
    row_index = bit_reverse + group_size * local_rows
    col_index = lax.iota(jnp.int32, length)
    real_part, imag_part = apply_kernel(real_part, imag_part, fresnel, row_index, col_index, length)
    back_re, back_im = angle_table(row_count, 1.0, row_count, row_count)
    real_part, imag_part = complex_mix("...lc,lm->...mc", real_part, imag_part, back_re, back_im)
    real_part = real_part / row_count
    imag_part = imag_part / row_count
    real_part, imag_part = (
        real_part * shift_re + imag_part * shift_im,
        imag_part * shift_re - real_part * shift_im,
    )
    for level in range(rounds):
        stride = 1 << level
        partner = swapped(jnp.stack((real_part, imag_part), axis=1), "rows", level)
        upper_flag = (position // stride % 2).astype(jnp.float32)
        within = (position % stride).astype(jnp.float32)
        phase_angle = 2.0 * math.pi / (2 * stride) * within
        turn_re = jnp.cos(phase_angle)
        turn_im = jnp.sin(phase_angle)
        lower_flag = 1.0 - upper_flag
        second_re = upper_flag * real_part + lower_flag * partner[:, 0]
        second_im = upper_flag * imag_part + lower_flag * partner[:, 1]
        first_re = upper_flag * partner[:, 0] + lower_flag * real_part
        first_im = upper_flag * partner[:, 1] + lower_flag * imag_part
        turned_re = second_re * turn_re - second_im * turn_im
        turned_im = second_re * turn_im + second_im * turn_re
        own_sign = 1.0 - 2.0 * upper_flag
        real_part = 0.5 * (first_re + own_sign * turned_re)
        imag_part = 0.5 * (first_im + own_sign * turned_im)
    real_part, imag_part = transform_last(real_part, imag_part, 1.0)
    real_part = real_part / length
    imag_part = imag_part / length
    return jnp.stack((real_part, imag_part), axis=1)


def solution(mesh):
    return jax.shard_map(
        body,
        mesh=mesh,
        in_specs=(P("dist", None, "rows", None), P(None, "rows", "dist"), P("dist")),
        out_specs=P("dist", None, "rows", None),
        check_vma=False,
    )
```

profile of v0, /device:TPU:97, one launch (start us, length us, event | category | flops | bytes accessed | tf_op | source)
XLA Modules:
  0.0 554.5 jit_solution(11762353641238578681)
XLA Ops:
  10.7 67.3 %all-gather.2.cloned.1.call-done = f32[2,128,2048]{1,2,0:T(8,128)} async-done(((f32[2,128,128]{1,2,0:T(8,128)}), f32[2,128,2048]{1,2,0:T(8,128)}) %all-gather.2.cloned.1.call-update) | async-done | bytes 2097168 | tf_op jit(solution)/shard_map/all_gather | solution.py:82
  78.0 5.1 fusion.24
  99.4 2.7 broadcast_multiply_fusion.1
  104.4 4.2 collective-permute-start
  108.7 88.3 %collective-permute-done = f32[1,2,128,2048]{3,2,1,0:T(8,128)} collective-permute-done((f32[1,2,128,2048]{3,2,1,0:T(8,128)}, f32[1,2,128,2048]{3,2,1,0:T(8,128)}, u32[]{:S(2)}, u32[]{:S(2)}) %collective-permute-start) | collective-permute-done | bytes 2097184 | tf_op jit(solution)/shard_map/ppermute | solution.py:11
  199.9 2.6 collective-permute-start.1
  202.7 40.7 %collective-permute-done.1 = f32[1,2,128,2048]{3,2,1,0:T(8,128)} collective-permute-done((f32[1,2,128,2048]{3,2,1,0:T(8,128)S(1)}, f32[1,2,128,2048]{3,2,1,0:T(8,128)}, u32[]{:S(2)}, u32[]{:S(2)}) %collective-permute-start.1) | collective-permute-done | bytes 2097184 | tf_op jit(solution)/shard_map/ppermute | solution.py:11
  248.6 39.9 %collective-permute-done.2 = f32[1,2,128,2048]{3,2,1,0:T(8,128)} collective-permute-done((f32[1,2,128,2048]{3,2,1,0:T(8,128)}, f32[1,2,128,2048]{3,2,1,0:T(8,128)}, u32[]{:S(2)}, u32[]{:S(2)}) %collective-permute-start.2) | collective-permute-done | bytes 2097184 | tf_op jit(solution)/shard_map/ppermute | solution.py:11
  292.0 7.2 %collective-permute-start.3 = (f32[1,2,128,2048]{3,2,1,0:T(8,128)}, f32[1,2,128,2048]{3,2,1,0:T(8,128)}, u32[]{:S(2)}, u32[]{:S(2)}) collective-permute-start(f32[1,2,128,2048]{3,2,1,0:T(8,128)} %pad_maximum_fusion.3), channel_id=1, source_target_pairs={{0,1},{1,0},{2,3},{3,2},{4,5},{5,4},{6,7},{7,6},{8,9},{9,8},{10,11... | collective-permute-start | bytes 6291464 | tf_op jit(solution)/shard_map/ppermute | solution.py:11
  302.2 2.8 bitcast_add_fusion.20
  315.1 5.5 fusion.57
  320.6 5.0 fusion.56
  325.6 5.2 convolution_subtract_fusion
  330.8 5.3 multiply_add_fusion
  336.4 4.1 collective-permute-done.4
  344.3 46.0 %collective-permute-done.5 = f32[1,2,128,2048]{3,2,1,0:T(8,128)} collective-permute-done((f32[1,2,128,2048]{3,2,1,0:T(8,128)}, f32[1,2,128,2048]{3,2,1,0:T(8,128)}, u32[]{:S(2)}, u32[]{:S(2)}) %collective-permute-start.5) | collective-permute-done | bytes 2097184 | tf_op jit(solution)/shard_map/ppermute | solution.py:11
  390.3 3.4 multiply_bitcast_fusion.3
  395.2 2.7 collective-permute-start.6
  398.0 45.1 %collective-permute-done.6 = f32[1,2,128,2048]{3,2,1,0:T(8,128)S(1)} collective-permute-done((f32[1,2,128,2048]{3,2,1,0:T(8,128)}, f32[1,2,128,2048]{3,2,1,0:T(8,128)S(1)}, u32[]{:S(2)}, u32[]{:S(2)}) %collective-permute-start.6) | collective-permute-done | bytes 2097184 | tf_op jit(solution)/shard_map/ppermute | solution.py:11
  444.4 2.7 multiply_bitcast_fusion.1
  448.5 3.6 collective-permute-start.7
  452.4 70.4 %collective-permute-done.7 = f32[1,2,128,2048]{3,2,1,0:T(8,128)} collective-permute-done((f32[1,2,128,2048]{3,2,1,0:T(8,128)}, f32[1,2,128,2048]{3,2,1,0:T(8,128)}, u32[]{:S(2)}, u32[]{:S(2)}) %collective-permute-start.7) | collective-permute-done | bytes 2097184 | tf_op jit(solution)/shard_map/ppermute | solution.py:11
  522.8 3.3 fusion.14
  532.3 2.9 fusion.5
  (70 shorter events, 72.8 us)
Async XLA Ops:
  6.5 71.5 %all-gather.2.cloned.1.call-start = ((), (), s32[]{:S(2)}) async-start(), calls=%async_computation | async-start | bytes 2228224 | tf_op jit(solution)/shard_map/all_gather | solution.py:82
  104.4 92.6 %collective-permute-start = (f32[1,2,128,2048]{3,2,1,0:T(8,128)}, f32[1,2,128,2048]{3,2,1,0:T(8,128)}, u32[]{:S(2)}, u32[]{:S(2)}) collective-permute-start(f32[1,2,128,2048]{3,2,1,0:T(8,128)} %pad_maximum_fusion), channel_id=1, source_target_pairs={{0,8},{1,9},{2,10},{3,11},{4,12},{5,13},{6,14},{7,15},{8,0},{9,1},... | collective-permute-start | bytes 6291464 | tf_op jit(solution)/shard_map/ppermute | solution.py:11
  198.9 1.0 copy-start
  199.9 43.5 %collective-permute-start.1 = (f32[1,2,128,2048]{3,2,1,0:T(8,128)S(1)}, f32[1,2,128,2048]{3,2,1,0:T(8,128)}, u32[]{:S(2)}, u32[]{:S(2)}) collective-permute-start(f32[1,2,128,2048]{3,2,1,0:T(8,128)S(1)} %pad_maximum_fusion.1), channel_id=1, source_target_pairs={{0,4},{1,5},{2,6},{3,7},{4,0},{5,1},{6,2},{7,3},{8,12},{9,13},{10,... | collective-permute-start | bytes 6291464 | tf_op jit(solution)/shard_map/ppermute | solution.py:11
  247.2 41.3 %collective-permute-start.2 = (f32[1,2,128,2048]{3,2,1,0:T(8,128)}, f32[1,2,128,2048]{3,2,1,0:T(8,128)}, u32[]{:S(2)}, u32[]{:S(2)}) collective-permute-start(f32[1,2,128,2048]{3,2,1,0:T(8,128)} %pad_maximum_fusion.2), channel_id=1, source_target_pairs={{0,2},{1,3},{2,0},{3,1},{4,6},{5,7},{6,4},{7,5},{8,10},{9,11},{10,... | collective-permute-start | bytes 6291464 | tf_op jit(solution)/shard_map/ppermute | solution.py:11
  290.5 9.5 %copy-start.1 = (f32[1,128,32,64]{1,2,3,0:T(8,128)S(1)}, f32[1,128,32,64]{1,2,3,0:T(8,128)}, u32[]{:S(2)}) copy-start(f32[1,128,32,64]{1,2,3,0:T(8,128)} %get-tuple-element.48) | copy-start | bytes 3145732
  292.0 13.1 %collective-permute-start.3 = (f32[1,2,128,2048]{3,2,1,0:T(8,128)}, f32[1,2,128,2048]{3,2,1,0:T(8,128)}, u32[]{:S(2)}, u32[]{:S(2)}) collective-permute-start(f32[1,2,128,2048]{3,2,1,0:T(8,128)} %pad_maximum_fusion.3), channel_id=1, source_target_pairs={{0,1},{1,0},{2,3},{3,2},{4,5},{5,4},{6,7},{7,6},{8,9},{9,8},{10,11... | collective-permute-start | bytes 6291464 | tf_op jit(solution)/shard_map/ppermute | solution.py:11
  300.0 1.2 copy-start.2
  336.3 4.2 collective-permute-start.4
  342.9 47.4 %collective-permute-start.5 = (f32[1,2,128,2048]{3,2,1,0:T(8,128)}, f32[1,2,128,2048]{3,2,1,0:T(8,128)}, u32[]{:S(2)}, u32[]{:S(2)}) collective-permute-start(f32[1,2,128,2048]{3,2,1,0:T(8,128)} %pad_maximum_fusion.5), channel_id=1, source_target_pairs={{0,2},{1,3},{2,0},{3,1},{4,6},{5,7},{6,4},{7,5},{8,10},{9,11},{10,... | collective-permute-start | bytes 6291464 | tf_op jit(solution)/shard_map/ppermute | solution.py:11
  395.2 47.9 %collective-permute-start.6 = (f32[1,2,128,2048]{3,2,1,0:T(8,128)}, f32[1,2,128,2048]{3,2,1,0:T(8,128)S(1)}, u32[]{:S(2)}, u32[]{:S(2)}) collective-permute-start(f32[1,2,128,2048]{3,2,1,0:T(8,128)} %pad_maximum_fusion.6), channel_id=1, source_target_pairs={{0,4},{1,5},{2,6},{3,7},{4,0},{5,1},{6,2},{7,3},{8,12},{9,13},{10,... | collective-permute-start | bytes 6291464 | tf_op jit(solution)/shard_map/ppermute | solution.py:11
  443.1 1.3 copy-start.3
  448.5 74.2 %collective-permute-start.7 = (f32[1,2,128,2048]{3,2,1,0:T(8,128)}, f32[1,2,128,2048]{3,2,1,0:T(8,128)}, u32[]{:S(2)}, u32[]{:S(2)}) collective-permute-start(f32[1,2,128,2048]{3,2,1,0:T(8,128)} %pad_maximum_fusion.7), channel_id=1, source_target_pairs={{0,8},{1,9},{2,10},{3,11},{4,12},{5,13},{6,14},{7,15},{8,0},{9,1},... | collective-permute-start | bytes 6291464 | tf_op jit(solution)/shard_map/ppermute | solution.py:11
Sparse Core Ops, SparseCore 0:
  9.1 68.7 all-gather.1
where the time goes:
time: 565 us; the launch traced here: 555 us
  waiting for transfers between devices  402 us (71%)
  matrix products  58.6 us (10%)
  other arithmetic  37.9 us (7%)
  starting transfers between devices  22.9 us (4%)
  local copies, waits for them, and re-layouts  17.4 us (3%)
  between operations  15.9 us (3%)
    ppermute x8, waiting for transfers between devices, swapped(): lax.ppermute(shard, axis, [(i, i ^ 1 << apart) for i in range(lax.axis_si...  334 us
    all_gather x1, waiting for transfers between devices, body(): slice_piece = lax.all_gather(object_slice, 'dist', axis=2, tiled=True)  67.3 us
    ppermute x8, starting transfers between devices, swapped(): lax.ppermute(shard, axis, [(i, i ^ 1 << apart) for i in range(lax.axis_si...  22.9 us
    dot_general x6, matrix products, complex_mix(): jnp.einsum(form, imag_part, table_im, precision=highest)  16.3 us
    another operation x11, other arithmetic, body(): partner = swapped(jnp.stack((real_part, imag_part), axis=1), 'rows', level)  16.2 us
    dot_general x6, matrix products, complex_mix(): jnp.einsum(form, imag_part, table_re, precision=highest)  14.8 us
    dot_general x6, matrix products, complex_mix(): jnp.einsum(form, real_part, table_re, precision=highest)  14 us
    dot_general x6, matrix products, complex_mix(): jnp.einsum(form, real_part, table_im, precision=highest)  13.5 us
  transfers between devices with their start and end apart: 9, of which 8 were waited for; matrix products, arithmetic and copies ran while one was open for 1% of the time, Pallas kernels for 0%

commit v1 on v0

--- a/solution.py
+++ b/solution.py
@@ -79,7 +79,9 @@
     length = wave.shape[3]
     group_size = lax.axis_size("rows")
     position = lax.axis_index("rows")
-    slice_piece = lax.all_gather(object_slice, "dist", axis=2, tiled=True)
+    slice_piece = jnp.concatenate(
+        lax.all_to_all(jnp.stack([object_slice] * lax.axis_size("dist")), "dist", 0, 0), axis=2
+    )
     amplitude = jnp.exp(-slice_piece[1])
     trans_re = amplitude * jnp.cos(slice_piece[0])
     trans_im = amplitude * jnp.sin(slice_piece[0])

time: 565 us -> 516 us (0.913)
  the two profiles are of different devices: /device:TPU:97 before, /device:TPU:52 now
where the time goes in v1:
time: 516 us; the launch traced here: 514 us
  waiting for transfers between devices  370 us (72%)
  matrix products  58.8 us (11%)
  other arithmetic  37.8 us (7%)
  local copies, waits for them, and re-layouts  23.2 us (4%)
  starting transfers between devices  21.7 us (4%)
    ppermute x8, waiting for transfers between devices, swapped(): lax.ppermute(shard, axis, [(i, i ^ 1 << apart) for i in range(lax.axis_si...  330 us
    all_to_all x1, waiting for transfers between devices, body(): lax.all_to_all(jnp.stack([object_slice] * lax.axis_size('dist')), 'dist',...  40.3 us
    dot_general x6, matrix products, complex_mix(): jnp.einsum(form, imag_part, table_im, precision=highest)  16.3 us
    another operation x11, other arithmetic, body(): partner = swapped(jnp.stack((real_part, imag_part), axis=1), 'rows', level)  16.2 us
    dot_general x6, matrix products, complex_mix(): jnp.einsum(form, imag_part, table_re, precision=highest)  15 us
    dot_general x6, matrix products, complex_mix(): jnp.einsum(form, real_part, table_re, precision=highest)  14 us
    dot_general x6, matrix products, complex_mix(): jnp.einsum(form, real_part, table_im, precision=highest)  13.5 us
    ppermute x8, starting transfers between devices, swapped(): lax.ppermute(shard, axis, [(i, i ^ 1 << apart) for i in range(lax.axis_si...  13.3 us
  transfers between devices with their start and end apart: 9, of which 8 were waited for; matrix products, arithmetic and copies ran while one was open for 2% of the time, Pallas kernels for 0%

profile of v1, /device:TPU:52, one launch (start us, length us, event | category | flops | bytes accessed | tf_op | source)
XLA Modules:
  0.0 513.6 jit_solution(9474873127654218339)
XLA Ops:
  2.6 8.4 %all-to-all-start = ((f32[16,2,128,128]{2,3,1,0:T(8,128)}), f32[16,2,128,128]{2,3,1,0:T(8,128)S(1)}, u32[]{:S(2)}, u32[]{:S(2)}) async-start(f32[16,2,128,128]{2,3,1,0:T(8,128)} %stack.36), calls=%async_computation | async-start | bytes 4194304 | tf_op jit(solution)/shard_map/all_to_all | solution.py:83
  11.0 3.1 fusion.250
  18.3 40.3 %all-to-all-done = f32[16,2,128,128]{2,3,1,0:T(8,128)S(1)} async-done(((f32[16,2,128,128]{2,3,1,0:T(8,128)}), f32[16,2,128,128]{2,3,1,0:T(8,128)S(1)}, u32[]{:S(2)}, u32[]{:S(2)}) %all-to-all-start) | async-done | bytes 2097184 | tf_op jit(solution)/shard_map/all_to_all | solution.py:83
  58.7 4.4 cosine_multiply_fusion
  74.0 2.8 broadcast_multiply_fusion
  80.0 2.7 broadcast_multiply_fusion.1
  85.1 4.4 collective-permute-start
  89.7 90.9 %collective-permute-done = f32[1,2,128,2048]{3,2,1,0:T(8,128)} collective-permute-done((f32[1,2,128,2048]{3,2,1,0:T(8,128)}, f32[1,2,128,2048]{3,2,1,0:T(8,128)}, u32[]{:S(2)}, u32[]{:S(2)}) %collective-permute-start) | collective-permute-done | bytes 2097184 | tf_op jit(solution)/shard_map/ppermute | solution.py:11
  184.2 48.5 %collective-permute-done.1 = f32[1,2,128,2048]{3,2,1,0:T(8,128)} collective-permute-done((f32[1,2,128,2048]{3,2,1,0:T(8,128)S(1)}, f32[1,2,128,2048]{3,2,1,0:T(8,128)}, u32[]{:S(2)}, u32[]{:S(2)}) %collective-permute-start.1) | collective-permute-done | bytes 2097184 | tf_op jit(solution)/shard_map/ppermute | solution.py:11
  237.7 45.7 %collective-permute-done.2 = f32[1,2,128,2048]{3,2,1,0:T(8,128)} collective-permute-done((f32[1,2,128,2048]{3,2,1,0:T(8,128)}, f32[1,2,128,2048]{3,2,1,0:T(8,128)}, u32[]{:S(2)}, u32[]{:S(2)}) %collective-permute-start.2) | collective-permute-done | bytes 2097184 | tf_op jit(solution)/shard_map/ppermute | solution.py:11
  290.1 2.8 bitcast_add_fusion.20
  303.0 5.5 %fusion.55 = f32[128,2048]{1,0:T(8,128)S(1)} fusion(f32[128,2048]{1,0:T(8,128)S(1)} %convolution_add_fusion.1, f32[128,2048]{1,0:T(8,128)S(1)} %convolution_subtract_fusion.1, f32[2048]{0:T(1024)S(1)} %fusion.123, f32[128]{0:T(128)S(1)} %get-tuple-element.52, f32[]{:T(128)} %bitcast.37), kind=kOutput, calls=%fused_computation.146 | convolution fusion | flops 404193280 | bytes 3154436 | tf_op jit(solution)/shard_map/...lc,lm->...mc/dot_general | solution.py:27
  308.5 5.0 fusion.54
  313.5 5.2 %convolution_subtract_fusion = f32[128,2048]{1,0:T(8,128)S(1)} fusion(f32[128,2048]{1,0:T(8,128)S(1)} %fusion.54, f32[128,2048]{1,0:T(8,128)S(1)} %convolution_add_fusion.1, f32[128,2048]{1,0:T(8,128)S(1)} %convolution_subtract_fusion.1, f32[2048]{0:T(1024)S(1)} %fusion.123, f32[128]{0:T(128)S(1)} %get-tuple-element.52, f32[]{:T(128)} %bitcast.37), kind=kOutput, calls=%fused_computation.1 | convolution fusion | flops 404455424 | bytes 4203012 | tf_op jit(solution)/shard_map/...lc,lm->...mc/dot_general | solution.py:24
  318.7 5.3 %multiply_add_fusion = (f32[128,2048]{1,0:T(8,128)S(1)}, f32[128,2048]{1,0:T(8,128)S(1)}) fusion(f32[128,2048]{1,0:T(8,128)S(1)} %convolution_subtract_fusion, f32[128]{0:T(128)S(1)} %get-tuple-element.54, f32[128]{0:T(128)S(1)} %get-tuple-element.55, f32[128,2048]{1,0:T(8,128)S(1)} %fusion.55, f32[128,2048]{1,0:T(8,128)S(1)} %convolution_add_fusion.1, ...), kind=kOutput, calls=%fused_computation.79 | convolution fusion | flops 406028288 | bytes 6301188 | tf_op jit(solution)/shard_map/...lc,lm->...mc/dot_general | solution.py:27
  324.7 3.8 collective-permute-done.4
  332.3 46.9 %collective-permute-done.5 = f32[1,2,128,2048]{3,2,1,0:T(8,128)} collective-permute-done((f32[1,2,128,2048]{3,2,1,0:T(8,128)}, f32[1,2,128,2048]{3,2,1,0:T(8,128)}, u32[]{:S(2)}, u32[]{:S(2)}) %collective-permute-start.5) | collective-permute-done | bytes 2097184 | tf_op jit(solution)/shard_map/ppermute | solution.py:11
  379.1 3.4 multiply_bitcast_fusion.3
  384.6 48.1 %collective-permute-done.6 = f32[1,2,128,2048]{3,2,1,0:T(8,128)S(1)} collective-permute-done((f32[1,2,128,2048]{3,2,1,0:T(8,128)}, f32[1,2,128,2048]{3,2,1,0:T(8,128)S(1)}, u32[]{:S(2)}, u32[]{:S(2)}) %collective-permute-start.6) | collective-permute-done | bytes 2097184 | tf_op jit(solution)/shard_map/ppermute | solution.py:11
  434.1 2.7 multiply_bitcast_fusion.1
  438.2 4.7 collective-permute-start.7
  443.2 45.7 %collective-permute-done.7 = f32[1,2,128,2048]{3,2,1,0:T(8,128)} collective-permute-done((f32[1,2,128,2048]{3,2,1,0:T(8,128)}, f32[1,2,128,2048]{3,2,1,0:T(8,128)}, u32[]{:S(2)}, u32[]{:S(2)}) %collective-permute-start.7) | collective-permute-done | bytes 2097184 | tf_op jit(solution)/shard_map/ppermute | solution.py:11
  488.8 3.3 fusion.14
  498.4 2.9 fusion.5
  (74 shorter events, 75.0 us)
Async XLA Ops:
  2.6 56.0 %all-to-all-start = ((f32[16,2,128,128]{2,3,1,0:T(8,128)}), f32[16,2,128,128]{2,3,1,0:T(8,128)S(1)}, u32[]{:S(2)}, u32[]{:S(2)}) async-start(f32[16,2,128,128]{2,3,1,0:T(8,128)} %stack.36), calls=%async_computation | async-start | bytes 4194304 | tf_op jit(solution)/shard_map/all_to_all | solution.py:83
  58.7 4.4 copy-start.3
  85.1 95.5 %collective-permute-start = (f32[1,2,128,2048]{3,2,1,0:T(8,128)}, f32[1,2,128,2048]{3,2,1,0:T(8,128)}, u32[]{:S(2)}, u32[]{:S(2)}) collective-permute-start(f32[1,2,128,2048]{3,2,1,0:T(8,128)} %pad_maximum_fusion), channel_id=1, source_target_pairs={{0,8},{1,9},{2,10},{3,11},{4,12},{5,13},{6,14},{7,15},{8,0},{9,1},... | collective-permute-start | bytes 6291464 | tf_op jit(solution)/shard_map/ppermute | solution.py:11
  182.5 1.0 copy-start
  183.5 49.2 %collective-permute-start.1 = (f32[1,2,128,2048]{3,2,1,0:T(8,128)S(1)}, f32[1,2,128,2048]{3,2,1,0:T(8,128)}, u32[]{:S(2)}, u32[]{:S(2)}) collective-permute-start(f32[1,2,128,2048]{3,2,1,0:T(8,128)S(1)} %pad_maximum_fusion.1), channel_id=1, source_target_pairs={{0,4},{1,5},{2,6},{3,7},{4,0},{5,1},{6,2},{7,3},{8,12},{9,13},{10,... | collective-permute-start | bytes 6291464 | tf_op jit(solution)/shard_map/ppermute | solution.py:11
  236.4 47.0 %collective-permute-start.2 = (f32[1,2,128,2048]{3,2,1,0:T(8,128)}, f32[1,2,128,2048]{3,2,1,0:T(8,128)}, u32[]{:S(2)}, u32[]{:S(2)}) collective-permute-start(f32[1,2,128,2048]{3,2,1,0:T(8,128)} %pad_maximum_fusion.2), channel_id=1, source_target_pairs={{0,2},{1,3},{2,0},{3,1},{4,6},{5,7},{6,4},{7,5},{8,10},{9,11},{10,... | collective-permute-start | bytes 6291464 | tf_op jit(solution)/shard_map/ppermute | solution.py:11
  285.4 2.5 copy-start.1
  286.8 6.1 %collective-permute-start.3 = (f32[1,2,128,2048]{3,2,1,0:T(8,128)}, f32[1,2,128,2048]{3,2,1,0:T(8,128)}, u32[]{:S(2)}, u32[]{:S(2)}) collective-permute-start(f32[1,2,128,2048]{3,2,1,0:T(8,128)} %pad_maximum_fusion.3), channel_id=1, source_target_pairs={{0,1},{1,0},{2,3},{3,2},{4,5},{5,4},{6,7},{7,6},{8,9},{9,8},{10,11... | collective-permute-start | bytes 6291464 | tf_op jit(solution)/shard_map/ppermute | solution.py:11
  287.9 1.2 copy-start.2
  324.2 4.3 collective-permute-start.4
  330.9 48.2 %collective-permute-start.5 = (f32[1,2,128,2048]{3,2,1,0:T(8,128)}, f32[1,2,128,2048]{3,2,1,0:T(8,128)}, u32[]{:S(2)}, u32[]{:S(2)}) collective-permute-start(f32[1,2,128,2048]{3,2,1,0:T(8,128)} %pad_maximum_fusion.5), channel_id=1, source_target_pairs={{0,2},{1,3},{2,0},{3,1},{4,6},{5,7},{6,4},{7,5},{8,10},{9,11},{10,... | collective-permute-start | bytes 6291464 | tf_op jit(solution)/shard_map/ppermute | solution.py:11
  383.9 48.8 %collective-permute-start.6 = (f32[1,2,128,2048]{3,2,1,0:T(8,128)}, f32[1,2,128,2048]{3,2,1,0:T(8,128)S(1)}, u32[]{:S(2)}, u32[]{:S(2)}) collective-permute-start(f32[1,2,128,2048]{3,2,1,0:T(8,128)} %pad_maximum_fusion.6), channel_id=1, source_target_pairs={{0,4},{1,5},{2,6},{3,7},{4,0},{5,1},{6,2},{7,3},{8,12},{9,13},{10,... | collective-permute-start | bytes 6291464 | tf_op jit(solution)/shard_map/ppermute | solution.py:11
  432.8 1.3 copy-start.4
  438.2 50.6 %collective-permute-start.7 = (f32[1,2,128,2048]{3,2,1,0:T(8,128)}, f32[1,2,128,2048]{3,2,1,0:T(8,128)}, u32[]{:S(2)}, u32[]{:S(2)}) collective-permute-start(f32[1,2,128,2048]{3,2,1,0:T(8,128)} %pad_maximum_fusion.7), channel_id=1, source_target_pairs={{0,8},{1,9},{2,10},{3,11},{4,12},{5,13},{6,14},{7,15},{8,0},{9,1},... | collective-permute-start | bytes 6291464 | tf_op jit(solution)/shard_map/ppermute | solution.py:11
